TPU v7x, 32 devices: a whole 2x2x4 slice. The times are simulated.
32 devices in a mesh: ctx: 8 (over z, x), chan: 4 (over y, core).
Axes of the slice: x: 2, y: 2, z: 4, core: 2. Of those that a mesh axis runs over, the one named last changes fastest.
Arguments:
- query_in: bfloat16 [4096, 1024], P('chan', 'ctx'), may hold values from -6 to 6
- key_in: bfloat16 [4096, 1024], P('chan', 'ctx'), may hold values from -6 to 6
- value_in: bfloat16 [4096, 1024], P('chan', 'ctx'), may hold values from -6 to 6
- short_kernel: float32 [3, 3, 4096], P(None, None, 'chan'), may hold values from -3.5 to 3.5
- filter_in: float32 [64, 64], replicated, may hold values from -0.75 to 0.75
- filter_out: float32 [64, 4096], P(None, 'chan'), may hold values from -0.75 to 0.75
- filter_decay: float32 [4096], P('chan'), may hold values from 0.5 to 40
- skip_gain: float32 [4096], P('chan'), may hold values from -3 to 3
- grad_out: bfloat16 [4096, 1024], P('chan', 'ctx'), may hold values from -6 to 6
Outputs:
- output: bfloat16 [4096, 1024], P('chan', 'ctx')
- grad_query: bfloat16 [4096, 1024], P('chan', 'ctx')
- grad_key: bfloat16 [4096, 1024], P('chan', 'ctx')
- grad_value: bfloat16 [4096, 1024], P('chan', 'ctx')
- grad_short: float32 [3, 3, 4096], P(None, None, 'chan')
- grad_filter_in: float32 [64, 64], replicated
- grad_filter_out: float32 [64, 4096], P(None, 'chan')
- grad_decay: float32 [4096], P('chan')
- grad_skip: float32 [4096], P('chan')
All inputs are finite; a program needn't handle non-finite values.
Results may differ from a plain program's by a relative error of at most 0.0006.
Values may be sent and summed in bfloat16 or wider, within the bound.
No kernel may reach another device: no remote copies, remote signals or barrier semaphores. Data moves between devices by JAX's collectives and lax.ppermute only.
A program may use at most 128 MiB of HBM per device.

v0:
```python
import math
import jax
import jax.numpy as jnp
from jax import lax
from jax.sharding import PartitionSpec as P

PRECISE = lax.Precision.HIGHEST


def shifted(value, axis, by):
    peers = lax.axis_size(axis)
    pairs = [(i, i + by) for i in range(peers) if 0 <= i + by < peers]
    return lax.ppermute(value, axis, pairs)


def position_features(position, sequence, feature_rows):
    bands = jnp.arange(feature_rows // 2, dtype=jnp.int32)
    factor = 4 * (bands + 1) * (bands + 1)
    phase = position[None, :] * factor[:, None] % sequence
    angles = 2.0 * math.pi / sequence * phase.astype(jnp.float32)
    return jnp.concatenate([jnp.cos(angles), jnp.sin(angles)], axis=0)


def angle_tables(left_index, right_index, modulus):
    phase = left_index[:, None] * right_index[None, :] % modulus
    angles = 2.0 * math.pi / modulus * phase.astype(jnp.float32)
    return (jnp.cos(angles), jnp.sin(angles))


def contract(form, left, right):
    return jnp.einsum(form, left, right, precision=PRECISE)


def times_forward(real_part, imag_part, cosine, sine):
    return (real_part * cosine + imag_part * sine, imag_part * cosine - real_part * sine)


def times_inverse(real_part, imag_part, cosine, sine):
    return (real_part * cosine - imag_part * sine, imag_part * cosine + real_part * sine)


def complex_times(first_real, first_imag, second_real, second_imag):
    return (
        first_real * second_real - first_imag * second_imag,
        first_real * second_imag + first_imag * second_real,
    )


def local_forward(real_part, imag_part):
    length = real_part.shape[-1]
    inner = 64
    outer = length // inner
    leading = real_part.shape[:-1]
    real_part = real_part.reshape(leading + (outer, inner))
    imag_part = imag_part.reshape(leading + (outer, inner))
    outer_index = jnp.arange(outer, dtype=jnp.int32)
    inner_index = jnp.arange(inner, dtype=jnp.int32)
    cos_outer, sin_outer = angle_tables(outer_index, outer_index, outer)
    first_real = contract("cb,...ba->...ca", cos_outer, real_part) + contract(
        "cb,...ba->...ca", sin_outer, imag_part
    )
    first_imag = contract("cb,...ba->...ca", cos_outer, imag_part) - contract(
        "cb,...ba->...ca", sin_outer, real_part
    )
    cos_middle, sin_middle = angle_tables(outer_index, inner_index, length)
    first_real, first_imag = times_forward(first_real, first_imag, cos_middle, sin_middle)
    cos_inner, sin_inner = angle_tables(inner_index, inner_index, inner)
    final_real = contract("...ca,da->...cd", first_real, cos_inner) + contract(
        "...ca,da->...cd", first_imag, sin_inner
    )
    final_imag = contract("...ca,da->...cd", first_imag, cos_inner) - contract(
        "...ca,da->...cd", first_real, sin_inner
    )
    return (final_real, final_imag)


def local_inverse(real_part, imag_part):
    outer = real_part.shape[-2]
    inner = real_part.shape[-1]
    length = outer * inner
    leading = real_part.shape[:-2]
    outer_index = jnp.arange(outer, dtype=jnp.int32)
    inner_index = jnp.arange(inner, dtype=jnp.int32)
    cos_inner, sin_inner = angle_tables(inner_index, inner_index, inner)
    first_real = contract("...cd,ad->...ca", real_part, cos_inner) - contract(
        "...cd,ad->...ca", imag_part, sin_inner
    )
    first_imag = contract("...cd,ad->...ca", imag_part, cos_inner) + contract(
        "...cd,ad->...ca", real_part, sin_inner
    )
    cos_middle, sin_middle = angle_tables(outer_index, inner_index, length)
    first_real, first_imag = times_inverse(first_real, first_imag, cos_middle, sin_middle)
    cos_outer, sin_outer = angle_tables(outer_index, outer_index, outer)
    final_real = contract("bc,...ca->...ba", cos_outer, first_real) - contract(
        "bc,...ca->...ba", sin_outer, first_imag
    )
    final_imag = contract("bc,...ca->...ba", cos_outer, first_imag) + contract(
        "bc,...ca->...ba", sin_outer, first_real
    )
    return (final_real.reshape(leading + (length,)), final_imag.reshape(leading + (length,)))


def held_frequencies(device):
    return 2 * device + jnp.arange(2, dtype=jnp.int32)


def forward_spectrum(signals):
    shards = lax.axis_size("ctx")
    device = lax.axis_index("ctx")
    signal_count, channels, length = signals.shape
    padded = 2 * shards * length
    columns = lax.all_to_all(
        signals.reshape((1, signal_count, channels, length)),
        "ctx",
        split_axis=3,
        concat_axis=0,
        tiled=True,
    )
    shard_index = jnp.arange(shards, dtype=jnp.int32)
    freq_index = jnp.arange(2 * shards, dtype=jnp.int32)
    cos_table, sin_table = angle_tables(freq_index, shard_index, 2 * shards)
    rows_real = contract("qp,pmgb->qmgb", cos_table, columns)
    rows_imag = -contract("qp,pmgb->qmgb", sin_table, columns)
    arrived = lax.all_to_all(
        jnp.stack([rows_real, rows_imag]), "ctx", split_axis=1, concat_axis=4, tiled=True
    )
    spec_real = arrived[0]
    spec_imag = arrived[1]
    freqs = held_frequencies(device)
    cosine, sine = angle_tables(freqs, jnp.arange(length, dtype=jnp.int32), padded)
    spec_real, spec_imag = times_forward(
        spec_real, spec_imag, cosine[:, None, None, :], sine[:, None, None, :]
    )
    return local_forward(spec_real, spec_imag)


def inverse_columns(spec_real, spec_imag):
    shards = lax.axis_size("ctx")
    device = lax.axis_index("ctx")
    real_part, imag_part = local_inverse(spec_real, spec_imag)
    length = real_part.shape[-1]
    padded = 2 * shards * length
    freqs = held_frequencies(device)
    cosine, sine = angle_tables(freqs, jnp.arange(length, dtype=jnp.int32), padded)
    real_part, imag_part = times_inverse(
        real_part, imag_part, cosine[:, None, None, :], sine[:, None, None, :]
    )
    shard_index = jnp.arange(shards, dtype=jnp.int32)
    arrived = lax.all_to_all(
        jnp.stack([real_part, imag_part]), "ctx", split_axis=4, concat_axis=1, tiled=True
    )
    cos_table, sin_table = angle_tables(
        shard_index, jnp.arange(2 * shards, dtype=jnp.int32), 2 * shards
    )
    columns = contract("pq,qmgb->pmgb", cos_table, arrived[0]) - contract(
        "pq,qmgb->pmgb", sin_table, arrived[1]
    )
    return columns * (1.0 / padded)


def to_tokens(columns):
    arrived = lax.all_to_all(columns, "ctx", split_axis=0, concat_axis=3, tiled=True)
    return arrived[0]


def body(
    query_in,
    key_in,
    value_in,
    short_kernel,
    filter_in,
    filter_out,
    filter_decay,
    skip_gain,
    grad_out,
):
    shards = lax.axis_size("ctx")
    device = lax.axis_index("ctx")
    length = query_in.shape[1]
    sequence = shards * length
    scale = sequence ** (-0.5)
    inputs = jnp.stack([query_in, key_in, value_in])
    rim = shifted(inputs[:, :, -2:], "ctx", 1)
    values = inputs.astype(jnp.float32)
    rim_values = rim.astype(jnp.float32)
    before_one = jnp.concatenate([rim_values[..., 1:], values[..., :-1]], axis=-1)
    before_two = jnp.concatenate([rim_values, values[..., :-2]], axis=-1)
    kernel = short_kernel[:, :, :, None]
    shorted = kernel[:, 0] * values + kernel[:, 1] * before_one + kernel[:, 2] * before_two
    query_short = shorted[0]
    key_short = shorted[1]
    value_short = shorted[2]
    gate = key_short * value_short
    position = device * length + jnp.arange(length, dtype=jnp.int32)
    fraction = position.astype(jnp.float32) / sequence
    basis = position_features(position, sequence, filter_in.shape[0])
    preact = jnp.dot(filter_in.T, basis, precision=PRECISE)
    hidden = jnp.sin(preact)
    window = jnp.exp(-filter_decay[:, None] * fraction[None, :])
    taps = window * jnp.dot(filter_out.T, hidden, precision=PRECISE) * scale
    spec_real, spec_imag = forward_spectrum(jnp.stack([gate, taps]))
    gate_real, gate_imag = (spec_real[:, 0], spec_imag[:, 0])
    taps_real, taps_imag = (spec_real[:, 1], spec_imag[:, 1])
    prod_real, prod_imag = complex_times(gate_real, gate_imag, taps_real, taps_imag)
    conv = to_tokens(inverse_columns(prod_real[:, None], prod_imag[:, None]))[0]
    mixed = conv + skip_gain[:, None] * gate
    output = (query_short * mixed).astype(jnp.bfloat16)
    upstream = grad_out.astype(jnp.float32)
    grad_mixed = upstream * query_short
    grad_query_short = upstream * mixed
    upper_real, upper_imag = forward_spectrum(grad_mixed[None])
    upper_real = upper_real[:, 0]
    upper_imag = upper_imag[:, 0]
    along_real, along_imag = complex_times(taps_real, -taps_imag, upper_real, upper_imag)
    cross_real, cross_imag = complex_times(gate_real, -gate_imag, upper_real, upper_imag)
    backward = to_tokens(
        inverse_columns(
            jnp.stack([along_real, cross_real], axis=1), jnp.stack([along_imag, cross_imag], axis=1)
        )
    )
    grad_gate = backward[0] + skip_gain[:, None] * grad_mixed
    grad_taps = backward[1]
    grads = jnp.stack([grad_query_short, grad_gate * value_short, grad_gate * key_short])
    after = shifted(grads[..., :2], "ctx", -1)
    next_one = jnp.concatenate([grads[..., 1:], after[..., :1]], axis=-1)
    next_two = jnp.concatenate([grads[..., 2:], after], axis=-1)
    grad_inputs = (kernel[:, 0] * grads + kernel[:, 1] * next_one + kernel[:, 2] * next_two).astype(
        jnp.bfloat16
    )
    short_terms = jnp.stack(
        [
            jnp.sum(grads * values, axis=-1),
            jnp.sum(grads * before_one, axis=-1),
            jnp.sum(grads * before_two, axis=-1),
        ],
        axis=1,
    )
    weighted = grad_taps * window * scale
    out_terms = jnp.dot(hidden, weighted.T, precision=PRECISE)
    grad_hidden = jnp.dot(filter_out, weighted, precision=PRECISE)
    in_terms = jnp.dot(basis, (grad_hidden * jnp.cos(preact)).T, precision=PRECISE)
    decay_terms = jnp.sum(grad_taps * taps * -fraction[None, :], axis=1)
    skip_terms = jnp.sum(grad_mixed * gate, axis=1)
    short_sum, out_sum, decay_sum, skip_sum = lax.psum(
        (short_terms, out_terms, decay_terms, skip_terms), "ctx"
    )
    in_sum = lax.psum(in_terms, ("ctx", "chan"))
    return (
        output,
        grad_inputs[0],
        grad_inputs[1],
        grad_inputs[2],
        short_sum * scale,
        in_sum * scale,
        out_sum * scale,
        decay_sum * scale,
        skip_sum * scale,
    )


def solution(mesh):
    placed = (
        P("chan", "ctx"),
        P("chan", "ctx"),
        P("chan", "ctx"),
        P(None, None, "chan"),
        P(),
        P(None, "chan"),
        P("chan"),
        P("chan"),
        P("chan", "ctx"),
    )
    return jax.shard_map(
        body,
        mesh=mesh,
        in_specs=placed,
        out_specs=(
            P("chan", "ctx"),
            P("chan", "ctx"),
            P("chan", "ctx"),
            P("chan", "ctx"),
            P(None, None, "chan"),
            P(),
            P(None, "chan"),
            P("chan"),
            P("chan"),
        ),
        check_vma=False,
    )
```

profile of v0, /device:TPU:0, one launch (start us, length us, event | category | flops | bytes accessed | tf_op | source)
XLA Modules:
  0.0 651.2 jit_solution(13803028707653949594)
XLA Ops:
  11.0 4.8 collective-permute-start
  20.5 6.6 %all-to-all-start.4 = ((f32[1,1,1024,128]{2,1,0,3:T(1,128)}), f32[1,1,1024,128]{2,1,0,3:T(1,128)}, u32[]{:S(2)}, u32[]{:S(2)}) async-start(f32[1,1,1024,128]{2,1,0,3:T(1,128)} %copy.246), calls=%async_computation.4 | async-start | bytes 1048576 | tf_op jit(solution)/shard_map/all_to_all | solution.py:112
  32.8 7.8 %all-to-all-done.4 = f32[1,1,1024,128]{2,1,0,3:T(1,128)} async-done(((f32[1,1,1024,128]{2,1,0,3:T(1,128)}), f32[1,1,1024,128]{2,1,0,3:T(1,128)}, u32[]{:S(2)}, u32[]{:S(2)}) %all-to-all-start.4) | async-done | bytes 524320 | tf_op jit(solution)/shard_map/all_to_all | solution.py:112
  40.6 4.2 all-to-all-start
  51.2 18.4 %all-to-all-done = f32[1,2,1024,128]{2,1,0,3:T(2,128)} async-done(((f32[1,2,1024,128]{2,1,0,3:T(2,128)}), f32[1,2,1024,128]{2,1,0,3:T(2,128)}, u32[]{:S(2)}, u32[]{:S(2)}) %all-to-all-start) | async-done | bytes 1048608 | tf_op jit(solution)/shard_map/all_to_all | solution.py:112
  69.6 4.8 all-to-all-start.5
  74.4 3.4 negate_bitcast_fusion
  77.9 3.4 convolution_bitcast_fusion
  81.9 4.4 copy.220
  86.3 35.7 %all-to-all-done.5 = f32[2,16,1,1024,16]{3,4,2,0,1:T(8,128)} async-done(((f32[2,16,1,1024,16]{3,4,2,0,1:T(8,128)}), f32[2,16,1,1024,16]{3,4,2,0,1:T(8,128)}, u32[]{:S(2)}, u32[]{:S(2)}) %all-to-all-start.5) | async-done | bytes 2097184 | tf_op jit(solution)/shard_map/all_to_all | solution.py:124
  122.0 4.7 all-to-all-start.1
  132.9 4.1 fusion.61
  136.9 4.3 fusion.35
  141.3 4.1 fusion.65
  145.3 5.7 subtract_bitcast_fusion.1
  157.5 61.7 %all-to-all-done.1 = f32[2,16,2,1024,16]{3,4,2,0,1:T(8,128)} async-done(((f32[2,16,2,1024,16]{3,4,2,0,1:T(8,128)}), f32[2,16,2,1024,16]{3,4,2,0,1:T(8,128)}, u32[]{:S(2)}, u32[]{:S(2)}) %all-to-all-start.1) | async-done | bytes 4194336 | tf_op jit(solution)/shard_map/all_to_all | solution.py:124
  224.1 7.9 %fusion.26 = f32[2,2,1024,64,2]{2,4,3,1,0:T(2,128)S(1)} fusion(f32[2,2,1024,2,64]{2,4,3,1,0:T(8,128)S(1)} %get-tuple-element.68), kind=kOutput, calls=%fused_computation.48 | convolution fusion | flops 12582968 | bytes 4194304 | tf_op jit(solution)/shard_map/cb,...ba->...ca/dot_general | solution.py:31
  232.0 8.3 %fusion.22 = f32[2,2,1024,64,2]{2,4,3,1,0:T(2,128)S(1)} fusion(f32[2,2,1024,2,64]{2,4,3,1,0:T(8,128)S(1)} %get-tuple-element.69), kind=kOutput, calls=%fused_computation.44 | convolution fusion | flops 12582968 | bytes 4194304 | tf_op jit(solution)/shard_map/cb,...ba->...ca/dot_general | solution.py:31
  240.3 8.2 %convolution_add_fusion = f32[2,2,1024,64,2]{2,4,3,1,0:T(2,128)S(1)} fusion(f32[2,2,1024,64,2]{2,4,3,1,0:T(2,128)S(1)} %fusion.26, f32[2,2,1024,2,64]{2,4,3,1,0:T(8,128)S(1)} %get-tuple-element.69), kind=kOutput, calls=%fused_computation.42 | convolution fusion | flops 13107256 | bytes 6291456 | tf_op jit(solution)/shard_map/cb,...ba->...ca/dot_general | solution.py:31
  248.6 11.2 %fusion.2 = (f32[2,2,1024,2,64]{2,3,4,1,0:T(2,128)S(1)}, f32[2,2,1024,2,64]{2,3,4,1,0:T(2,128)S(1)}) fusion(f32[2,2,1024,64,2]{2,4,3,1,0:T(2,128)S(1)} %convolution_add_fusion, f32[2,64]{0,1:T(8,128)S(1)} %copy-done.21, f32[2,64]{0,1:T(8,128)S(1)} %copy-done.23, f32[2,2,1024,64,2]{2,4,3,1,0:T(2,128)S(1)} %fusion.22, ...), kind=kOutput, calls=%fused_computation.14 | convolution fusion | flops 16252984 | bytes 10486784 | tf_op jit(solution)/shard_map/cb,...ba->...ca/dot_general | solution.py:31
  265.4 3.1 fusion.16
  268.6 3.1 fusion.19
  271.7 3.9 multiply_subtract_fusion.3
  284.9 9.6 %multiply_subtract_fusion = (f32[2,2,1024,2,64]{2,3,4,1,0:T(2,128)S(1)}, f32[2,2,1024,2,64]{2,3,4,1,0:T(2,128)S(1)}) fusion(f32[2,64]{0,1:T(8,128)S(1)} %copy-done.21, f32[2,64]{0,1:T(8,128)S(1)} %copy-done.23, f32[2,2,1024,2,64]{2,4,3,1,0:T(8,128)S(1)} %fusion.13, f32[2,2,1024,2,64]{2,4,3,1,0:T(8,128)S(1)} %fusion.15, ...), kind=kLoop, calls=%fused_computation.23 | loop fusion | flops 4194304 | bytes 12583936 | tf_op jit(solution)/shard_map/sub | solution.py:39
  294.5 7.5 %fusion.190 = f32[2,2,1024,64,2]{2,4,3,1,0:T(2,128)S(1)} fusion(f32[2,2,1024,2,64]{2,3,4,1,0:T(2,128)S(1)} %get-tuple-element.60), kind=kOutput, calls=%fused_computation.283 | convolution fusion | flops 12582968 | bytes 4194304 | tf_op jit(solution)/shard_map/bc,...ca->...ba/dot_general | solution.py:31
  302.0 7.5 %fusion.188 = f32[2,2,1024,64,2]{2,4,3,1,0:T(2,128)S(1)} fusion(f32[2,2,1024,2,64]{2,3,4,1,0:T(2,128)S(1)} %get-tuple-element.61), kind=kOutput, calls=%fused_computation.281 | convolution fusion | flops 12582968 | bytes 4194304 | tf_op jit(solution)/shard_map/bc,...ca->...ba/dot_general | solution.py:31
  309.6 8.4 %subtract_bitcast_fusion = f32[2,2,1024,2,64]{2,3,4,1,0:T(2,128)S(1)} fusion(f32[2,2,1024,64,2]{2,4,3,1,0:T(2,128)S(1)} %fusion.190, f32[2,2,1024,2,64]{2,3,4,1,0:T(2,128)S(1)} %get-tuple-element.61), kind=kOutput, calls=%fused_computation.21 | convolution fusion | flops 13107256 | bytes 6291456 | tf_op jit(solution)/shard_map/bc,...ca->...ba/dot_general | solution.py:31
  317.9 8.0 %add_bitcast_fusion = f32[2,2,1024,2,64]{2,3,4,1,0:T(2,128)S(1)} fusion(f32[2,2,1024,64,2]{2,4,3,1,0:T(2,128)S(1)} %fusion.188, f32[2,2,1024,2,64]{2,3,4,1,0:T(2,128)S(1)} %get-tuple-element.60), kind=kOutput, calls=%fused_computation.20 | convolution fusion | flops 13107256 | bytes 6291456 | tf_op jit(solution)/shard_map/bc,...ca->...ba/dot_general | solution.py:31
  328.8 5.2 copy.268
  334.0 5.0 all-to-all-start.6
  345.8 4.1 fusion.67
  349.8 4.3 fusion.37
  354.5 4.1 fusion.71
  358.5 4.4 fusion.38
  366.8 64.8 %all-to-all-done.6 = f32[2,2,2,1024,128]{3,2,1,0,4:T(2,128)} async-done(((f32[2,2,2,1024,128]{3,2,1,0,4:T(2,128)}), f32[2,2,2,1024,128]{3,2,1,0,4:T(2,128)}, u32[]{:S(2)}, u32[]{:S(2)}) %all-to-all-start.6) | async-done | bytes 4194336 | tf_op jit(solution)/shard_map/all_to_all | solution.py:149
  431.5 4.4 all-to-all-start.2
  435.9 4.6 copy.269
  445.3 3.7 squeeze.65
  449.1 4.6 copy.270
  453.7 3.7 squeeze.64
  462.9 20.8 %all-to-all-done.2 = f32[2,2,1,1024,128]{3,1,2,0,4:T(2,128)} async-done(((f32[2,2,1,1024,128]{3,1,2,0,4:T(2,128)}), f32[2,2,1,1024,128]{3,1,2,0,4:T(2,128)}, u32[]{:S(2)}, u32[]{:S(2)}) %all-to-all-start.2) | async-done | bytes 2097184 | tf_op jit(solution)/shard_map/all_to_all | solution.py:149
  483.7 4.5 all-to-all-start.7
  496.9 3.0 copy.242
  506.5 7.3 %all-to-all-done.7 = f32[8,2,1024,16]{2,3,1,0:T(8,128)} async-done(((f32[8,2,1024,16]{2,3,1,0:T(8,128)}), f32[8,2,1024,16]{2,3,1,0:T(8,128)}, u32[]{:S(2)}, u32[]{:S(2)}) %all-to-all-start.7) | async-done | bytes 1048608 | tf_op jit(solution)/shard_map/all_to_all | solution.py:162
  513.8 4.1 all-to-all-start.3
  523.4 40.9 %psum.36 = f32[64,64]{1,0:T(8,128)S(1)} all-reduce(f32[64,64]{1,0:T(8,128)} %fusion.105), channel_id=1, replica_groups=mesh['ctx'=8,'chan'=4] {'ctx','chan'}, use_global_device_ids=true, to_apply=%region_4.5 | all-reduce | flops 4096 | bytes 32768 | tf_op jit(solution)/shard_map/psum | solution.py:247
  574.1 37.3 %all-reduce = (f32[3,3,1024]{2,0,1:T(4,128)S(1)}, f32[1024]{0:T(1024)S(1)}, f32[1024]{0:T(1024)S(1)}) all-reduce(f32[3,3,1024]{2,0,1:T(4,128)S(1)} %pad_maximum_fusion.14, f32[1024]{0:T(1024)S(1)} %get-tuple-element.106, f32[1024]{0:T(1024)S(1)} %get-tuple-element.96), channel_id=1, replica_groups=mesh['ctx'=8,'chan'=4] {'ctx'}, use_global_device_ids=true, to_apply=%region_3.4 | all-reduce | flops 11264 | bytes 90112 | tf_op jit(solution)/shard_map/psum | solution.py:244
  621.0 21.3 %all-reduce.3.cloned.1.call-done = f32[64,1024]{1,0:T(8,128)} async-done(((f32[64,1024]{1,0:T(8,128)}), f32[64,1024]{1,0:T(8,128)}) %all-reduce.3.cloned.1.call-update) | async-done | bytes 262160 | tf_op jit(solution)/shard_map/psum | solution.py:244
  (188 shorter events, 118.8 us)
Async XLA Ops:
  7.2 22.2 %copy-start = (f32[64,1024]{1,0:T(8,128)S(1)}, f32[64,1024]{1,0:T(8,128)}, u32[]{:S(2)}) copy-start(f32[64,1024]{1,0:T(8,128)} %param.14) | copy-start | bytes 786436
  8.3 2.6 copy-start.10
  8.3 7.5 %copy-start.27 = (f32[3,3,1024]{2,1,0:T(4,128)S(1)}, f32[3,3,1024]{2,1,0:T(4,128)}, u32[]{:S(2)}) copy-start(f32[3,3,1024]{2,1,0:T(4,128)} %param.12) | copy-start | bytes 110596
  8.3 7.7 %copy-start.36 = (f32[1024]{0:T(1024)S(1)}, f32[1024]{0:T(1024)}, u32[]{:S(2)}) copy-start(f32[1024]{0:T(1024)} %param.15) | copy-start | bytes 12292
  8.4 7.8 %copy-start.19 = (bf16[1024,128]{1,0:T(8,128)(2,1)S(1)}, bf16[1024,128]{1,0:T(8,128)(2,1)}, u32[]{:S(2)}) copy-start(bf16[1024,128]{1,0:T(8,128)(2,1)} %param.17) | copy-start | bytes 786436
  9.6 7.4 %copy-start.11 = (bf16[1024,128]{0,1:T(8,128)(2,1)}, bf16[1024,128]{0,1:T(8,128)(2,1)S(1)}, u32[]{:S(2)}) copy-start(bf16[1024,128]{0,1:T(8,128)(2,1)S(1)} %copy.215) | copy-start | bytes 786436
  10.8 6.5 copy-start.12
  11.0 6.2 collective-permute-start
  17.3 1.8 copy-start.25
  17.3 1.7 copy-start.18
  20.5 20.0 %all-to-all-start.4 = ((f32[1,1,1024,128]{2,1,0,3:T(1,128)}), f32[1,1,1024,128]{2,1,0,3:T(1,128)}, u32[]{:S(2)}, u32[]{:S(2)}) async-start(f32[1,1,1024,128]{2,1,0,3:T(1,128)} %copy.246), calls=%async_computation.4 | async-start | bytes 1048576 | tf_op jit(solution)/shard_map/all_to_all | solution.py:112
  27.7 1.7 copy-start.37
  30.1 0.8 copy-start.8
  40.6 29.0 %all-to-all-start = ((f32[1,2,1024,128]{2,1,0,3:T(2,128)}), f32[1,2,1024,128]{2,1,0,3:T(2,128)}, u32[]{:S(2)}, u32[]{:S(2)}) async-start(f32[1,2,1024,128]{2,1,0,3:T(2,128)} %copy.217), calls=%async_computation | async-start | bytes 2097152 | tf_op jit(solution)/shard_map/all_to_all | solution.py:112
  69.6 52.4 %all-to-all-start.5 = ((f32[2,16,1,1024,16]{3,4,2,0,1:T(8,128)}), f32[2,16,1,1024,16]{3,4,2,0,1:T(8,128)}, u32[]{:S(2)}, u32[]{:S(2)}) async-start(f32[2,16,1,1024,16]{3,4,2,0,1:T(8,128)} %copy.248), calls=%async_computation.5 | async-start | bytes 4194304 | tf_op jit(solution)/shard_map/all_to_all | solution.py:124
  122.0 97.3 %all-to-all-start.1 = ((f32[2,16,2,1024,16]{3,4,2,0,1:T(8,128)}), f32[2,16,2,1024,16]{3,4,2,0,1:T(8,128)}, u32[]{:S(2)}, u32[]{:S(2)}) async-start(f32[2,16,2,1024,16]{3,4,2,0,1:T(8,128)} %copy.220), calls=%async_computation.1 | async-start | bytes 8388608 | tf_op jit(solution)/shard_map/all_to_all | solution.py:124
  127.4 2.1 copy-start.30
  130.3 2.2 copy-start.28
  141.2 4.1 copy-start.20
  141.2 4.1 copy-start.22
  151.1 4.0 copy-start.15
  222.6 0.7 copy-start.29
  240.3 8.3 %copy-start.21 = (f32[2,64]{0,1:T(8,128)S(1)}, f32[2,64]{0,1:T(8,128)}, u32[]{:S(2)}) copy-start(f32[2,64]{0,1:T(8,128)} %copy.229) | copy-start | bytes 1540
  240.3 8.3 %copy-start.23 = (f32[2,64]{0,1:T(8,128)S(1)}, f32[2,64]{0,1:T(8,128)}, u32[]{:S(2)}) copy-start(f32[2,64]{0,1:T(8,128)} %copy.226) | copy-start | bytes 1540
  268.5 3.1 copy-start.14
  268.6 3.1 copy-start.16
  268.6 3.1 copy-start.17
  326.5 0.7 copy-start.33
  334.0 97.5 %all-to-all-start.6 = ((f32[2,2,2,1024,128]{3,2,1,0,4:T(2,128)}), f32[2,2,2,1024,128]{3,2,1,0,4:T(2,128)}, u32[]{:S(2)}, u32[]{:S(2)}) async-start(f32[2,2,2,1024,128]{3,2,1,0,4:T(2,128)} %copy.268), calls=%async_computation.6 | async-start | bytes 8388608 | tf_op jit(solution)/shard_map/all_to_all | solution.py:149
  339.0 2.6 copy-start.1
  339.0 3.8 copy-start.2
  342.9 1.3 copy-start.31
  342.9 1.3 copy-start.32
  358.5 4.7 copy-start.35
  431.5 52.2 %all-to-all-start.2 = ((f32[2,2,1,1024,128]{3,1,2,0,4:T(2,128)}), f32[2,2,1,1024,128]{3,1,2,0,4:T(2,128)}, u32[]{:S(2)}, u32[]{:S(2)}) async-start(f32[2,2,1,1024,128]{3,1,2,0,4:T(2,128)} %copy.240), calls=%async_computation.2 | async-start | bytes 4194304 | tf_op jit(solution)/shard_map/all_to_all | solution.py:149
  457.3 2.9 copy-start.3
  483.7 30.1 %all-to-all-start.7 = ((f32[8,2,1024,16]{2,3,1,0:T(8,128)}), f32[8,2,1024,16]{2,3,1,0:T(8,128)}, u32[]{:S(2)}, u32[]{:S(2)}) async-start(f32[8,2,1024,16]{2,3,1,0:T(8,128)} %copy.272), calls=%async_computation.7 | async-start | bytes 2097152 | tf_op jit(solution)/shard_map/all_to_all | solution.py:162
  502.8 2.0 copy-start.13
  513.8 53.3 %all-to-all-start.3 = ((f32[8,1,1024,16]{2,3,1,0:T(8,128)}), f32[8,1,1024,16]{2,3,1,0:T(8,128)}, u32[]{:S(2)}, u32[]{:S(2)}) async-start(f32[8,1,1024,16]{2,3,1,0:T(8,128)} %copy.244), calls=%async_computation.3 | async-start | bytes 1048576 | tf_op jit(solution)/shard_map/all_to_all | solution.py:162
  517.9 124.3 %all-reduce.3.cloned.1.call-start = ((), (), s32[]{:S(2)}) async-start(), calls=%async_computation.8 | async-start | bytes 524288 | tf_op jit(solution)/shard_map/psum | solution.py:244
  518.0 2.2 copy-start.9
  518.0 3.9 copy-start.24
  521.1 0.8 copy-start.7
  567.0 4.7 copy-start.26
  612.0 5.7 collective-permute-start.1
  614.1 3.7 copy-start.4
  614.1 3.7 copy-start.5
  614.1 3.7 copy-start.6
  (1 other events, 0.7 us)
Sparse Core Ops, SparseCore 0:
  571.8 70.4 all-reduce.2
where the time goes:
time: 659 us; the launch traced here: 651 us
  waiting for transfers between devices  241 us (37%)
  matrix products  162 us (25%)
  local copies, waits for them, and re-layouts  82.3 us (12%)
  blocking collectives  78.2 us (12%)
  starting transfers between devices  44.5 us (7%)
  other arithmetic  28.1 us (4%)
  between operations  15.7 us (2%)
    dot_general x40, matrix products, contract(): return jnp.einsum(form, left, right, precision=PRECISE)  156 us
    all_to_all x2, waiting for transfers between devices, forward_spectrum(): lax.all_to_all(jnp.stack([rows_real, rows_imag]), 'ctx', split_axis=1, co...  97.4 us
    all_to_all x2, waiting for transfers between devices, inverse_columns(): lax.all_to_all(jnp.stack([real_part, imag_part]), 'ctx', split_axis=4, co...  85.6 us
    psum x1, blocking collectives, body(): in_sum = lax.psum(in_terms, ('ctx', 'chan'))  40.9 us
    psum x1, blocking collectives, body(): lax.psum((short_terms, out_terms, decay_terms, skip_terms), 'ctx')  37.3 us
    all_to_all x2, waiting for transfers between devices, forward_spectrum(): lax.all_to_all(signals.reshape((1, signal_count, channels, length)), 'ctx...  26.2 us
    psum x1, waiting for transfers between devices, body(): lax.psum((short_terms, out_terms, decay_terms, skip_terms), 'ctx')  21.3 us
  transfers between devices with their start and end apart: 11, of which 10 were waited for; matrix products, arithmetic and copies ran while one was open for 22% of the time, Pallas kernels for 0%

commit v1 on v0

--- a/solution.py
+++ b/solution.py
@@ -244,7 +244,7 @@
     short_sum, out_sum, decay_sum, skip_sum = lax.psum(
         (short_terms, out_terms, decay_terms, skip_terms), "ctx"
     )
-    in_sum = lax.psum(in_terms, ("ctx", "chan"))
+    in_sum = lax.psum(lax.psum(in_terms, "chan"), "ctx")
     return (
         output,
         grad_inputs[0],

time: 659 us -> 631 us (0.958)
  blocking collectives: 78.2 us -> 49.7 us
    psum x1, blocking collectives: 40.9 us -> 11.2 us  [body(): in_sum = lax.psum(lax.psum(in_terms, 'chan'), 'ctx')]
  transfers between devices with their start and end apart: 11 -> 11, of which waited for: 10 -> 10; matrix products, arithmetic and copies ran while one was open for 22% -> 23% of each run, Pallas kernels for 0% -> 0%
where the time goes in v1:
time: 631 us; the launch traced here: 623 us
  waiting for transfers between devices  240 us (38%)
  matrix products  162 us (26%)
  local copies, waits for them, and re-layouts  82.3 us (13%)
  blocking collectives  49.7 us (8%)
  starting transfers between devices  44.5 us (7%)
  other arithmetic  28.1 us (4%)
  between operations  15.7 us (2%)
    dot_general x40, matrix products, contract(): return jnp.einsum(form, left, right, precision=PRECISE)  156 us
    all_to_all x2, waiting for transfers between devices, forward_spectrum(): lax.all_to_all(jnp.stack([rows_real, rows_imag]), 'ctx', split_axis=1, co...  97.4 us
    all_to_all x2, waiting for transfers between devices, inverse_columns(): lax.all_to_all(jnp.stack([real_part, imag_part]), 'ctx', split_axis=4, co...  85.6 us
    psum x1, blocking collectives, body(): lax.psum((short_terms, out_terms, decay_terms, skip_terms), 'ctx')  38.6 us
    all_to_all x2, waiting for transfers between devices, forward_spectrum(): lax.all_to_all(signals.reshape((1, signal_count, channels, length)), 'ctx...  26.2 us
    psum x1, waiting for transfers between devices, body(): lax.psum((short_terms, out_terms, decay_terms, skip_terms), 'ctx')  21.1 us
    unnamed x88, local copies, waits for them, and re-layouts  12.7 us
  transfers between devices with their start and end apart: 11, of which 10 were waited for; matrix products, arithmetic and copies ran while one was open for 23% of the time, Pallas kernels for 0%

profile of v1, /device:TPU:0, one launch (start us, length us, event | category | flops | bytes accessed | tf_op | source)
XLA Modules:
  0.0 622.5 jit_solution(553772671685644068)
XLA Ops:
  11.0 4.8 collective-permute-start
  20.5 6.6 %all-to-all-start.4 = ((f32[1,1,1024,128]{2,1,0,3:T(1,128)}), f32[1,1,1024,128]{2,1,0,3:T(1,128)}, u32[]{:S(2)}, u32[]{:S(2)}) async-start(f32[1,1,1024,128]{2,1,0,3:T(1,128)} %copy.246), calls=%async_computation.4 | async-start | bytes 1048576 | tf_op jit(solution)/shard_map/all_to_all | solution.py:112
  32.8 7.8 %all-to-all-done.4 = f32[1,1,1024,128]{2,1,0,3:T(1,128)} async-done(((f32[1,1,1024,128]{2,1,0,3:T(1,128)}), f32[1,1,1024,128]{2,1,0,3:T(1,128)}, u32[]{:S(2)}, u32[]{:S(2)}) %all-to-all-start.4) | async-done | bytes 524320 | tf_op jit(solution)/shard_map/all_to_all | solution.py:112
  40.6 4.2 all-to-all-start
  51.2 18.4 %all-to-all-done = f32[1,2,1024,128]{2,1,0,3:T(2,128)} async-done(((f32[1,2,1024,128]{2,1,0,3:T(2,128)}), f32[1,2,1024,128]{2,1,0,3:T(2,128)}, u32[]{:S(2)}, u32[]{:S(2)}) %all-to-all-start) | async-done | bytes 1048608 | tf_op jit(solution)/shard_map/all_to_all | solution.py:112
  69.6 4.8 all-to-all-start.5
  74.4 3.4 negate_bitcast_fusion
  77.9 3.4 convolution_bitcast_fusion
  81.9 4.4 copy.220
  86.3 35.7 %all-to-all-done.5 = f32[2,16,1,1024,16]{3,4,2,0,1:T(8,128)} async-done(((f32[2,16,1,1024,16]{3,4,2,0,1:T(8,128)}), f32[2,16,1,1024,16]{3,4,2,0,1:T(8,128)}, u32[]{:S(2)}, u32[]{:S(2)}) %all-to-all-start.5) | async-done | bytes 2097184 | tf_op jit(solution)/shard_map/all_to_all | solution.py:124
  122.0 4.7 all-to-all-start.1
  132.9 4.1 fusion.61
  136.9 4.3 fusion.35
  141.3 4.1 fusion.65
  145.3 5.7 subtract_bitcast_fusion.1
  157.5 61.7 %all-to-all-done.1 = f32[2,16,2,1024,16]{3,4,2,0,1:T(8,128)} async-done(((f32[2,16,2,1024,16]{3,4,2,0,1:T(8,128)}), f32[2,16,2,1024,16]{3,4,2,0,1:T(8,128)}, u32[]{:S(2)}, u32[]{:S(2)}) %all-to-all-start.1) | async-done | bytes 4194336 | tf_op jit(solution)/shard_map/all_to_all | solution.py:124
  224.1 7.9 %fusion.26 = f32[2,2,1024,64,2]{2,4,3,1,0:T(2,128)S(1)} fusion(f32[2,2,1024,2,64]{2,4,3,1,0:T(8,128)S(1)} %get-tuple-element.69), kind=kOutput, calls=%fused_computation.48 | convolution fusion | flops 12582968 | bytes 4194304 | tf_op jit(solution)/shard_map/cb,...ba->...ca/dot_general | solution.py:31
  232.0 8.3 %fusion.22 = f32[2,2,1024,64,2]{2,4,3,1,0:T(2,128)S(1)} fusion(f32[2,2,1024,2,64]{2,4,3,1,0:T(8,128)S(1)} %get-tuple-element.70), kind=kOutput, calls=%fused_computation.44 | convolution fusion | flops 12582968 | bytes 4194304 | tf_op jit(solution)/shard_map/cb,...ba->...ca/dot_general | solution.py:31
  240.3 8.2 %convolution_add_fusion = f32[2,2,1024,64,2]{2,4,3,1,0:T(2,128)S(1)} fusion(f32[2,2,1024,64,2]{2,4,3,1,0:T(2,128)S(1)} %fusion.26, f32[2,2,1024,2,64]{2,4,3,1,0:T(8,128)S(1)} %get-tuple-element.70), kind=kOutput, calls=%fused_computation.42 | convolution fusion | flops 13107256 | bytes 6291456 | tf_op jit(solution)/shard_map/cb,...ba->...ca/dot_general | solution.py:31
  248.6 11.2 %fusion.2 = (f32[2,2,1024,2,64]{2,3,4,1,0:T(2,128)S(1)}, f32[2,2,1024,2,64]{2,3,4,1,0:T(2,128)S(1)}) fusion(f32[2,2,1024,64,2]{2,4,3,1,0:T(2,128)S(1)} %convolution_add_fusion, f32[2,64]{0,1:T(8,128)S(1)} %copy-done.21, f32[2,64]{0,1:T(8,128)S(1)} %copy-done.23, f32[2,2,1024,64,2]{2,4,3,1,0:T(2,128)S(1)} %fusion.22, ...), kind=kOutput, calls=%fused_computation.14 | convolution fusion | flops 16252984 | bytes 10486784 | tf_op jit(solution)/shard_map/cb,...ba->...ca/dot_general | solution.py:31
  265.4 3.1 fusion.16
  268.6 3.1 fusion.19
  271.7 3.9 multiply_subtract_fusion.3
  284.9 9.6 %multiply_subtract_fusion = (f32[2,2,1024,2,64]{2,3,4,1,0:T(2,128)S(1)}, f32[2,2,1024,2,64]{2,3,4,1,0:T(2,128)S(1)}) fusion(f32[2,64]{0,1:T(8,128)S(1)} %copy-done.21, f32[2,64]{0,1:T(8,128)S(1)} %copy-done.23, f32[2,2,1024,2,64]{2,4,3,1,0:T(8,128)S(1)} %fusion.13, f32[2,2,1024,2,64]{2,4,3,1,0:T(8,128)S(1)} %fusion.15, ...), kind=kLoop, calls=%fused_computation.23 | loop fusion | flops 4194304 | bytes 12583936 | tf_op jit(solution)/shard_map/sub | solution.py:39
  294.5 7.5 %fusion.190 = f32[2,2,1024,64,2]{2,4,3,1,0:T(2,128)S(1)} fusion(f32[2,2,1024,2,64]{2,3,4,1,0:T(2,128)S(1)} %get-tuple-element.61), kind=kOutput, calls=%fused_computation.283 | convolution fusion | flops 12582968 | bytes 4194304 | tf_op jit(solution)/shard_map/bc,...ca->...ba/dot_general | solution.py:31
  302.0 7.5 %fusion.188 = f32[2,2,1024,64,2]{2,4,3,1,0:T(2,128)S(1)} fusion(f32[2,2,1024,2,64]{2,3,4,1,0:T(2,128)S(1)} %get-tuple-element.62), kind=kOutput, calls=%fused_computation.281 | convolution fusion | flops 12582968 | bytes 4194304 | tf_op jit(solution)/shard_map/bc,...ca->...ba/dot_general | solution.py:31
  309.6 8.4 %subtract_bitcast_fusion = f32[2,2,1024,2,64]{2,3,4,1,0:T(2,128)S(1)} fusion(f32[2,2,1024,64,2]{2,4,3,1,0:T(2,128)S(1)} %fusion.190, f32[2,2,1024,2,64]{2,3,4,1,0:T(2,128)S(1)} %get-tuple-element.62), kind=kOutput, calls=%fused_computation.21 | convolution fusion | flops 13107256 | bytes 6291456 | tf_op jit(solution)/shard_map/bc,...ca->...ba/dot_general | solution.py:31
  317.9 8.0 %add_bitcast_fusion = f32[2,2,1024,2,64]{2,3,4,1,0:T(2,128)S(1)} fusion(f32[2,2,1024,64,2]{2,4,3,1,0:T(2,128)S(1)} %fusion.188, f32[2,2,1024,2,64]{2,3,4,1,0:T(2,128)S(1)} %get-tuple-element.61), kind=kOutput, calls=%fused_computation.20 | convolution fusion | flops 13107256 | bytes 6291456 | tf_op jit(solution)/shard_map/bc,...ca->...ba/dot_general | solution.py:31
  328.8 5.2 copy.268
  334.0 5.0 all-to-all-start.6
  345.8 4.1 fusion.67
  349.8 4.3 fusion.37
  354.5 4.1 fusion.71
  358.5 4.4 fusion.38
  366.8 64.8 %all-to-all-done.6 = f32[2,2,2,1024,128]{3,2,1,0,4:T(2,128)} async-done(((f32[2,2,2,1024,128]{3,2,1,0,4:T(2,128)}), f32[2,2,2,1024,128]{3,2,1,0,4:T(2,128)}, u32[]{:S(2)}, u32[]{:S(2)}) %all-to-all-start.6) | async-done | bytes 4194336 | tf_op jit(solution)/shard_map/all_to_all | solution.py:149
  431.5 4.4 all-to-all-start.2
  435.9 4.6 copy.269
  445.3 3.7 squeeze.65
  449.1 4.6 copy.270
  453.7 3.7 squeeze.64
  462.9 20.8 %all-to-all-done.2 = f32[2,2,1,1024,128]{3,1,2,0,4:T(2,128)} async-done(((f32[2,2,1,1024,128]{3,1,2,0,4:T(2,128)}), f32[2,2,1,1024,128]{3,1,2,0,4:T(2,128)}, u32[]{:S(2)}, u32[]{:S(2)}) %all-to-all-start.2) | async-done | bytes 2097184 | tf_op jit(solution)/shard_map/all_to_all | solution.py:149
  483.7 4.5 all-to-all-start.7
  496.9 3.0 copy.242
  506.5 7.3 %all-to-all-done.7 = f32[8,2,1024,16]{2,3,1,0:T(8,128)} async-done(((f32[8,2,1024,16]{2,3,1,0:T(8,128)}), f32[8,2,1024,16]{2,3,1,0:T(8,128)}, u32[]{:S(2)}, u32[]{:S(2)}) %all-to-all-start.7) | async-done | bytes 1048608 | tf_op jit(solution)/shard_map/all_to_all | solution.py:162
  513.8 4.1 all-to-all-start.3
  523.4 11.2 %psum.43 = f32[64,64]{1,0:T(8,128)S(1)} all-reduce(f32[64,64]{1,0:T(8,128)} %fusion.105), channel_id=1, replica_groups=mesh['ctx'=8,'chan'=4] {'chan'}, use_global_device_ids=true, to_apply=%region_4.5 | all-reduce | flops 4096 | bytes 32768 | tf_op jit(solution)/shard_map/psum | solution.py:247
  543.8 38.6 %all-reduce = (f32[3,3,1024]{2,0,1:T(4,128)S(1)}, f32[64,64]{1,0:T(8,128)S(1)}, f32[1024]{0:T(1024)S(1)}, f32[1024]{0:T(1024)S(1)}) all-reduce(f32[3,3,1024]{2,0,1:T(4,128)S(1)} %pad_maximum_fusion.14, f32[64,64]{1,0:T(8,128)S(1)} %psum.43, f32[1024]{0:T(1024)S(1)} %get-tuple-element.106, ...), channel_id=1, replica_groups=mesh['ctx'=8,'chan'=4] {'ctx'}, use_global_device_ids=true, to_apply=%region_3.4 | all-reduce | flops 15360 | bytes 122880 | tf_op jit(solution)/shard_map/psum | solution.py:244
  592.5 21.1 %all-reduce.3.cloned.1.call-done = f32[64,1024]{1,0:T(8,128)} async-done(((f32[64,1024]{1,0:T(8,128)}), f32[64,1024]{1,0:T(8,128)}) %all-reduce.3.cloned.1.call-update) | async-done | bytes 262160 | tf_op jit(solution)/shard_map/psum | solution.py:244
  (188 shorter events, 118.8 us)
Async XLA Ops:
  7.2 22.2 %copy-start = (f32[64,1024]{1,0:T(8,128)S(1)}, f32[64,1024]{1,0:T(8,128)}, u32[]{:S(2)}) copy-start(f32[64,1024]{1,0:T(8,128)} %param.14) | copy-start | bytes 786436
  8.3 2.6 copy-start.10
  8.3 7.5 %copy-start.27 = (f32[3,3,1024]{2,1,0:T(4,128)S(1)}, f32[3,3,1024]{2,1,0:T(4,128)}, u32[]{:S(2)}) copy-start(f32[3,3,1024]{2,1,0:T(4,128)} %param.12) | copy-start | bytes 110596
  8.3 7.7 %copy-start.36 = (f32[1024]{0:T(1024)S(1)}, f32[1024]{0:T(1024)}, u32[]{:S(2)}) copy-start(f32[1024]{0:T(1024)} %param.15) | copy-start | bytes 12292
  8.4 7.8 %copy-start.19 = (bf16[1024,128]{1,0:T(8,128)(2,1)S(1)}, bf16[1024,128]{1,0:T(8,128)(2,1)}, u32[]{:S(2)}) copy-start(bf16[1024,128]{1,0:T(8,128)(2,1)} %param.17) | copy-start | bytes 786436
  9.6 7.4 %copy-start.11 = (bf16[1024,128]{0,1:T(8,128)(2,1)}, bf16[1024,128]{0,1:T(8,128)(2,1)S(1)}, u32[]{:S(2)}) copy-start(bf16[1024,128]{0,1:T(8,128)(2,1)S(1)} %copy.215) | copy-start | bytes 786436
  10.8 6.5 %copy-start.12 = (bf16[1024,128]{0,1:T(8,128)(2,1)}, bf16[1024,128]{0,1:T(8,128)(2,1)S(1)}, u32[]{:S(2)}) copy-start(bf16[1024,128]{0,1:T(8,128)(2,1)S(1)} %copy.216) | copy-start | bytes 786436
  11.0 6.2 %collective-permute-start = (bf16[3,1024,2]{1,2,0:T(2,128)(2,1)S(1)}, bf16[3,1024,2]{1,2,0:T(2,128)(2,1)S(1)}, u32[]{:S(2)}, u32[]{:S(2)}) collective-permute-start(bf16[3,1024,2]{1,2,0:T(2,128)(2,1)S(1)} %slice.139), channel_id=1, source_target_pairs={{0,4},{4,8},{8,12},{12,16},{16,20},{20,24},{24,28},{1,5},{5,9},{9,... | collective-permute-start | bytes 36872 | tf_op jit(solution)/shard_map/ppermute | solution.py:13
  17.3 1.8 copy-start.25
  17.3 1.7 copy-start.18
  20.5 20.0 %all-to-all-start.4 = ((f32[1,1,1024,128]{2,1,0,3:T(1,128)}), f32[1,1,1024,128]{2,1,0,3:T(1,128)}, u32[]{:S(2)}, u32[]{:S(2)}) async-start(f32[1,1,1024,128]{2,1,0,3:T(1,128)} %copy.246), calls=%async_computation.4 | async-start | bytes 1048576 | tf_op jit(solution)/shard_map/all_to_all | solution.py:112
  27.7 1.7 copy-start.37
  30.1 0.8 copy-start.8
  40.6 29.0 %all-to-all-start = ((f32[1,2,1024,128]{2,1,0,3:T(2,128)}), f32[1,2,1024,128]{2,1,0,3:T(2,128)}, u32[]{:S(2)}, u32[]{:S(2)}) async-start(f32[1,2,1024,128]{2,1,0,3:T(2,128)} %copy.217), calls=%async_computation | async-start | bytes 2097152 | tf_op jit(solution)/shard_map/all_to_all | solution.py:112
  69.6 52.4 %all-to-all-start.5 = ((f32[2,16,1,1024,16]{3,4,2,0,1:T(8,128)}), f32[2,16,1,1024,16]{3,4,2,0,1:T(8,128)}, u32[]{:S(2)}, u32[]{:S(2)}) async-start(f32[2,16,1,1024,16]{3,4,2,0,1:T(8,128)} %copy.248), calls=%async_computation.5 | async-start | bytes 4194304 | tf_op jit(solution)/shard_map/all_to_all | solution.py:124
  122.0 97.3 %all-to-all-start.1 = ((f32[2,16,2,1024,16]{3,4,2,0,1:T(8,128)}), f32[2,16,2,1024,16]{3,4,2,0,1:T(8,128)}, u32[]{:S(2)}, u32[]{:S(2)}) async-start(f32[2,16,2,1024,16]{3,4,2,0,1:T(8,128)} %copy.220), calls=%async_computation.1 | async-start | bytes 8388608 | tf_op jit(solution)/shard_map/all_to_all | solution.py:124
  127.4 2.1 copy-start.30
  130.3 2.2 copy-start.28
  141.2 4.1 copy-start.20
  141.2 4.1 copy-start.22
  151.1 4.0 copy-start.15
  222.6 0.7 copy-start.29
  240.3 8.3 %copy-start.21 = (f32[2,64]{0,1:T(8,128)S(1)}, f32[2,64]{0,1:T(8,128)}, u32[]{:S(2)}) copy-start(f32[2,64]{0,1:T(8,128)} %copy.229) | copy-start | bytes 1540
  240.3 8.3 %copy-start.23 = (f32[2,64]{0,1:T(8,128)S(1)}, f32[2,64]{0,1:T(8,128)}, u32[]{:S(2)}) copy-start(f32[2,64]{0,1:T(8,128)} %copy.226) | copy-start | bytes 1540
  268.5 3.1 copy-start.14
  268.6 3.1 copy-start.16
  268.6 3.1 copy-start.17
  326.5 0.7 copy-start.33
  334.0 97.5 %all-to-all-start.6 = ((f32[2,2,2,1024,128]{3,2,1,0,4:T(2,128)}), f32[2,2,2,1024,128]{3,2,1,0,4:T(2,128)}, u32[]{:S(2)}, u32[]{:S(2)}) async-start(f32[2,2,2,1024,128]{3,2,1,0,4:T(2,128)} %copy.268), calls=%async_computation.6 | async-start | bytes 8388608 | tf_op jit(solution)/shard_map/all_to_all | solution.py:149
  339.0 2.6 copy-start.1
  339.0 3.8 copy-start.2
  342.9 1.3 copy-start.31
  342.9 1.3 copy-start.32
  358.5 4.7 copy-start.35
  431.5 52.2 %all-to-all-start.2 = ((f32[2,2,1,1024,128]{3,1,2,0,4:T(2,128)}), f32[2,2,1,1024,128]{3,1,2,0,4:T(2,128)}, u32[]{:S(2)}, u32[]{:S(2)}) async-start(f32[2,2,1,1024,128]{3,1,2,0,4:T(2,128)} %copy.240), calls=%async_computation.2 | async-start | bytes 4194304 | tf_op jit(solution)/shard_map/all_to_all | solution.py:149
  457.3 2.9 copy-start.3
  483.7 30.1 %all-to-all-start.7 = ((f32[8,2,1024,16]{2,3,1,0:T(8,128)}), f32[8,2,1024,16]{2,3,1,0:T(8,128)}, u32[]{:S(2)}, u32[]{:S(2)}) async-start(f32[8,2,1024,16]{2,3,1,0:T(8,128)} %copy.272), calls=%async_computation.7 | async-start | bytes 2097152 | tf_op jit(solution)/shard_map/all_to_all | solution.py:162
  502.8 2.0 copy-start.13
  513.8 22.9 %all-to-all-start.3 = ((f32[8,1,1024,16]{2,3,1,0:T(8,128)}), f32[8,1,1024,16]{2,3,1,0:T(8,128)}, u32[]{:S(2)}, u32[]{:S(2)}) async-start(f32[8,1,1024,16]{2,3,1,0:T(8,128)} %copy.244), calls=%async_computation.3 | async-start | bytes 1048576 | tf_op jit(solution)/shard_map/all_to_all | solution.py:162
  517.9 95.7 %all-reduce.3.cloned.1.call-start = ((), (), s32[]{:S(2)}) async-start(), calls=%async_computation.8 | async-start | bytes 524288 | tf_op jit(solution)/shard_map/psum | solution.py:244
  518.0 2.2 copy-start.9
  518.0 3.9 copy-start.24
  521.1 0.8 copy-start.7
  536.7 4.7 copy-start.26
  583.6 5.7 collective-permute-start.1
  585.6 3.7 copy-start.4
  585.6 3.7 copy-start.5
  585.7 3.7 copy-start.6
  (1 other events, 0.7 us)
Sparse Core Ops, SparseCore 0:
  541.5 72.0 all-reduce.2
